TPU v7x, 32 devices: a whole 2x2x4 slice. The times are simulated.
32 devices in a mesh: seq: 16 (over z, x, core), tp: 2 (over y).
Axes of the slice: x: 2, y: 2, z: 4, core: 2. Of those that a mesh axis runs over, the one named last changes fastest.
Arguments:
- tokens: bfloat16 [256, 8192], P('tp', 'seq'), may hold values from -6 to 6
- gate_weight: bfloat16 [8192, 14336], P('seq', 'tp'), may hold values from -0.0625 to 0.0625
- up_weight: bfloat16 [8192, 14336], P('seq', 'tp'), may hold values from -0.0625 to 0.0625
- down_weight: bfloat16 [14336, 8192], P('tp', 'seq'), may hold values from -0.09375 to 0.09375
- masks: int32 [2, 112], P(None, 'tp'), may hold values from 0 to 1, as said below
- cotangent: bfloat16 [256, 8192], P('tp', 'seq'), may hold values from -6 to 6
Outputs:
- output: bfloat16 [256, 8192], P('tp', 'seq')
- grad_tokens: bfloat16 [256, 8192], P('tp', 'seq')
- grad_gate: float32 [8192, 14336], P('seq', 'tp')
- grad_up: float32 [8192, 14336], P('seq', 'tp')
- grad_down: float32 [14336, 8192], P('tp', 'seq')
Inputs may be any that keep to these rules, and one draw needn't show every extreme that they name: Each row of masks holds exactly 28 ones. Cut a row into 2 groups of 56 consecutive blocks: in every row one group holds exactly 28 ones, and the remaining ones are spread over the other groups as evenly as possible, so that their counts differ by at most one.
All inputs are finite; a program needn't handle non-finite values.
Results may differ from a plain program's by a relative error of at most 0.0049.
Values may be sent and summed in bfloat16 or wider, within the bound.
A program may use at most 192 MiB of HBM per device.

v0:
```python
import functools
import math

import jax
import jax.numpy as jnp
from jax import lax
from jax.experimental import pallas as pl
from jax.experimental.pallas import tpu as pltpu
from jax.sharding import PartitionSpec as P

BLK = 128
ROWBLK = 128
KEEP_PART = 4
MESH = pl.DeviceIdType.MESH
PLAIN_LIMIT = 20 * 1024 * 1024
COMM_LIMIT = 28 * 1024 * 1024
WIDE_LIMIT = 60 * 1024 * 1024
FUSED_LIMIT = 60 * 1024 * 1024


def group_of(count):
    for size in (7, 8, 4, 2):
        if count % size == 0:
            return size
    return 1


def wide_group(count):
    for size in (7, 8, 4, 2):
        if count % size == 0:
            return size
    return 1


def tables_kernel(capacity, first_ref, mask_ref, table_ref, index_ref, case_ref):
    row_blocks, blocks = mask_ref.shape
    sources = [lax.rem(first_ref[0] + row, row_blocks) for row in range(row_blocks)]

    def clear(slot, carry):
        for row in range(row_blocks):
            table_ref[row, slot] = -1
            index_ref[row, slot] = 0
        return carry

    lax.fori_loop(0, capacity + 1, clear, 0, unroll=True)

    def step(block, taken):
        following = []
        for row in range(row_blocks):
            kept = mask_ref[sources[row], block]
            at = jnp.minimum(taken[row], capacity)
            table_ref[row, at] = jnp.where(kept == 1, block, -1)
            index_ref[row, at] = jnp.where(kept == 1, block, 0)
            table_ref[row, capacity + 1 + block] = jnp.where(kept == 1, at, -1)
            following.append(taken[row] + kept)
        return tuple(following)

    counts = lax.fori_loop(0, blocks, step, (jnp.int32(0),) * row_blocks, unroll=8)
    for row in range(row_blocks):
        index_ref[row, capacity] = jnp.minimum(counts[row], 1)
    mine, other = counts[0] > 0, counts[row_blocks - 1] > 0
    case_ref[0] = jnp.where(mine == other, 2, jnp.where(mine, 0, 1))


def unit_tables(masks, first, capacity):
    row_blocks, blocks = masks.shape
    smem = pl.BlockSpec(memory_space=pltpu.SMEM)
    return pl.pallas_call(
        functools.partial(tables_kernel, capacity),
        out_shape=(
            jax.ShapeDtypeStruct((row_blocks, capacity + 1 + blocks), jnp.int32),
            jax.ShapeDtypeStruct((row_blocks, capacity + 1), jnp.int32),
            jax.ShapeDtypeStruct((1,), jnp.int32),
        ),
        in_specs=[smem, smem],
        out_specs=(smem, smem, smem),
    )(first.reshape(1), masks)


def rows_kernel(count, tok_ref, cot_ref, tok_all, cot_all, send_sem, recv_sem, own_sem):
    me = lax.axis_index("tp")
    barrier = pltpu.get_barrier_semaphore()
    for shift in range(1, count):
        pl.semaphore_signal(
            barrier, inc=1, device_id={"tp": lax.rem(me + shift, count)}, device_id_type=MESH
        )
    pl.semaphore_wait(barrier, count - 1)
    copies = []
    for which, (src, dst) in enumerate(((tok_ref, tok_all), (cot_ref, cot_all))):
        for shift in range(1, count):
            copy = pltpu.make_async_remote_copy(
                src_ref=src,
                dst_ref=dst.at[me],
                send_sem=send_sem.at[which, shift],
                recv_sem=recv_sem.at[which, shift],
                device_id={"tp": lax.rem(me + shift, count)},
                device_id_type=MESH,
            )
            copy.start()
            copies.append(copy)
        own = pltpu.make_async_copy(src, dst.at[me], own_sem.at[which])
        own.start()
        copies.append(own)
    for copy in copies:
        copy.wait()


def gather_rows(tokens, cotangent):
    count = lax.axis_size("tp")
    rows, feats = tokens.shape
    anywhere = pl.BlockSpec(memory_space=pl.ANY)
    return pl.pallas_call(
        functools.partial(rows_kernel, count),
        out_shape=(jax.ShapeDtypeStruct((count, rows, feats), tokens.dtype),) * 2,
        in_specs=[anywhere] * 2,
        out_specs=(anywhere,) * 2,
        scratch_shapes=[
            pltpu.SemaphoreType.DMA((2, count)),
            pltpu.SemaphoreType.DMA((2, count)),
            pltpu.SemaphoreType.DMA((2,)),
        ],
        compiler_params=pltpu.CompilerParams(collective_id=0, has_side_effects=True),
    )(tokens, cotangent)


def parts_kernel(first, group, table_ref, tok_ref, cot_ref, *refs):
    gates, ups, downs = refs[:group], refs[group : 2 * group], refs[2 * group : 3 * group]
    out_ref = refs[3 * group]
    row, step = pl.program_id(0) + first, pl.program_id(1)
    tok, cot = tok_ref[...], cot_ref[...]
    for at in range(group):
        live = table_ref[row, step * group + at] >= 0
        rows = slice(at * ROWBLK, (at + 1) * ROWBLK)
        both = jnp.dot(
            tok,
            jnp.concatenate([gates[at][...], ups[at][...]], axis=1),
            preferred_element_type=jnp.float32,
        )
        grad = lax.dot_general(
            cot, downs[at][...], (((1,), (1,)), ((), ())), preferred_element_type=jnp.float32
        )
        out_ref[0, rows, :] = both[:, :BLK]
        out_ref[1, rows, :] = jnp.where(live, both[:, BLK:], 0.0)
        out_ref[2, rows, :] = jnp.where(live, grad, 0.0)


def weight_specs(first, group, feats):
    def block(table, row, step, at):
        return jnp.maximum(table[row + first, step * group + at], 0)

    def columns(at):
        return pl.BlockSpec((feats, BLK), lambda row, step, table: (0, block(table, row, step, at)))

    def rows(at):
        return pl.BlockSpec((BLK, feats), lambda row, step, table: (block(table, row, step, at), 0))

    return (
        [columns(at) for at in range(group)] * 2 + [rows(at) for at in range(group)]
    )


def partial_products(table, first, capacity, tok, cot, gate_w, up_w, down_w):
    row_blocks, feats = tok.shape[0] // ROWBLK, tok.shape[1]
    group = group_of(capacity)
    steps = capacity // group
    rows_spec = pl.BlockSpec((ROWBLK, feats), lambda row, step, table: (row, 0))
    flops = 6 * row_blocks * ROWBLK * feats * capacity * BLK
    return pl.pallas_call(
        functools.partial(parts_kernel, first, group),
        out_shape=jax.ShapeDtypeStruct((3, row_blocks * capacity * ROWBLK, BLK), jnp.float32),
        grid_spec=pltpu.PrefetchScalarGridSpec(
            num_scalar_prefetch=1,
            grid=(row_blocks, steps),
            in_specs=[rows_spec, rows_spec] + weight_specs(first, group, feats),
            out_specs=pl.BlockSpec(
                (3, group * ROWBLK, BLK), lambda row, step, table: (0, row * steps + step, 0)
            ),
        ),
        compiler_params=pltpu.CompilerParams(vmem_limit_bytes=PLAIN_LIMIT),
        cost_estimate=pl.CostEstimate(
            flops=flops, bytes_accessed=flops // ROWBLK, transcendentals=0
        ),
    )(table, tok, cot, *([gate_w] * group + [up_w] * group + [down_w] * group))


def exchange_kernel(
    count, inputs, *refs
):
    part_refs, all_ref = refs[:inputs], refs[inputs]
    (
        mine, paired, xsend, xland, zsend, zland, acts,
        load_sem, pair_send, pair_recv, x_send, x_recv, z_send, z_recv,
    up_send, down_send, side_send, all_recv, hand_send, hand_recv, own_sem,
    ) = refs[inputs + 1 :]
    _, _, subs, wide, tall, _, _ = part_refs[0].shape
    halves = inputs * subs
    chips = count // 2
    me = lax.axis_index("seq")
    chip, core = me // 2, lax.rem(me, 2)
    sibling = {"seq": me + 1 - 2 * core}
    along, across = chip // wide, lax.rem(chip, wide)
    order = sorted(range(1, tall), key=lambda shift: abs(2 * shift - tall))

    def device(i, j):
        return {"seq": (i * wide + j) * 2 + core}

    def column(shift):
        return lax.rem(across + shift, wide)

    def line(shift):
        return lax.rem(along + shift, tall)

    def remote(src, dst, send, recv, target):
        return pltpu.make_async_remote_copy(
            src_ref=src, dst_ref=dst, send_sem=send, recv_sem=recv,
            device_id=target, device_id_type=MESH,
        )

    barrier = pltpu.get_barrier_semaphore()
    pl.semaphore_signal(barrier, inc=1, device_id=sibling, device_id_type=MESH)
    for s in range(1, wide):
        pl.semaphore_signal(
            barrier, inc=1, device_id=device(along, column(s)), device_id_type=MESH
        )
    for d in range(1, tall):
        pl.semaphore_signal(barrier, inc=1, device_id=device(line(d), across), device_id_type=MESH)
    pl.semaphore_wait(barrier, wide + tall - 1)

    def part_at(h, s, d, side):
        return part_refs[h // subs].at[:, side, h % subs, column(s), line(d)]

    def load_copy(h, s, d):
        return pltpu.make_async_copy(
            part_at(h, s, d, core), mine.at[h, s, d], load_sem.at[h, s, d]
        )

    def pair_copy(h, s, d):
        return remote(
            part_at(h, s, d, 1 - core), paired.at[h, s, d],
            pair_send.at[h, s, d], pair_recv.at[h, s, d], sibling,
        )

    def x_copy(h, s, d):
        return remote(
            xsend.at[h, s - 1, d], xland.at[h, s - 1, d],
            x_send.at[h, s, d], x_recv.at[h, s, d], device(along, column(s)),
        )

    def z_copy(h, d):
        return remote(
            zsend.at[h, d - 1], zland.at[h, d - 1],
            z_send.at[h, d], z_recv.at[h, d], device(line(d), across),
        )

    def slot(h, i, j, side):
        return all_ref.at[h // subs, :, side, h % subs, j, i]

    def z_route(h, i, j, to, send, src=None):
        dst = slot(h, i, j, core)
        owner = i * wide + j
        return remote(
            dst if src is None else src, dst, send.at[h, owner], all_recv.at[h, owner],
            device(to, across),
        )

    def x_route(h, i, s, src=None):
        dst = slot(h, i, across, core)
        return remote(
            dst if src is None else src, dst, side_send.at[h, s, i],
            all_recv.at[h, i * wide + across], device(along, column(s)),
        )

    def hand_copy(h, i, j, side, src=None):
        dst = slot(h, i, j, side)
        owner = i * wide + j
        return remote(
            dst if src is None else src, dst, hand_send.at[h, owner], hand_recv.at[h, owner], sibling
        )

    def take(h, i, j):
        z_route(h, i, j, along, up_send).wait_recv()

    def pass_on(h, i, j, up, down, src=None):
        if up:

            @pl.when(along < tall - 1)
            def _():
                z_route(h, i, j, along + 1, up_send, src).start()

        if down:

            @pl.when(along > 0)
            def _():
                z_route(h, i, j, along - 1, down_send, src).start()

    def spread(h, i, src=None):
        for s in range(1, wide):
            x_route(h, i, s, src).start()

    for h in range(halves):
        for s in list(range(1, wide)) + [0]:
            for d in order + [0]:
                pair_copy(h, s, d).start()
                load_copy(h, s, d).start()

    for h in range(halves):
        for d in order + [0]:
            for s in range(1, wide):
                load_copy(h, s, d).wait()
                pair_copy(h, s, d).wait_recv()
                xsend[h, s - 1, d] = (mine[h, s, d] + paired[h, s, d]).astype(jnp.bfloat16)
                x_copy(h, s, d).start()

    def row_sum(h, d):
        load_copy(h, 0, d).wait()
        pair_copy(h, 0, d).wait_recv()
        total = mine[h, 0, d] + paired[h, 0, d]
        for s in range(1, wide):
            x_copy(h, s, d).wait_recv()
            total = total + xland[h, s - 1, d].astype(jnp.float32)
        return total

    for h in range(halves):
        for d in order:
            zsend[h, d - 1] = row_sum(h, d).astype(jnp.bfloat16)
            z_copy(h, d).start()

    def own_copy(h):
        return pltpu.make_async_copy(acts.at[h], slot(h, along, across, core), own_sem.at[h])

    for h in range(halves):
        total = row_sum(h, 0)
        for d in order:
            z_copy(h, d).wait_recv()
            total = total + zland[h, d - 1].astype(jnp.float32)
        gate, up, grad = total[0], total[1], total[2]
        sig = jax.nn.sigmoid(gate)
        acts[h, 0] = (gate * sig * up).astype(jnp.bfloat16)
        acts[h, 1] = (grad * up * sig * (1.0 + gate * (1.0 - sig))).astype(jnp.bfloat16)
        acts[h, 2] = (grad * gate * sig).astype(jnp.bfloat16)
        src = acts.at[h]
        pass_on(h, along, across, True, True, src)
        spread(h, along, src)
        hand_copy(h, along, across, core, src).start()
        own_copy(h).start()

    for h in range(halves):
        if h % 2 == 1:
            for s in range(1, wide):
                take(h, along, column(s))
                pass_on(h, along, column(s), True, True)
                hand_copy(h, along, column(s), core).start()
    for far in range(1, tall):
        for h in range(halves):
            for s in range(wide if h % 2 == 1 else 1):
                for sign in (-1, 1):

                    @pl.when(along >= far if sign < 0 else along + far < tall)
                    def _(h=h, s=s, sign=sign):
                        i = along + sign * far
                        take(h, i, column(s))
                        pass_on(h, i, column(s), sign < 0, sign > 0)
                        if h % 2 == 0:
                            spread(h, i)
                        hand_copy(h, i, column(s), core).start()

    for h in range(0, halves, 2):
        for s in range(1, wide):
            for d in [0] + list(range(1, tall)):
                take(h, line(d), column(s))
                hand_copy(h, line(d), column(s), core).start()

    for h in range(halves):
        own_copy(h).wait()

        def finish(owner, carry, h=h):
            i, j = owner // wide, lax.rem(owner, wide)
            hand_copy(h, i, j, 1 - core).wait_recv()
            hand_copy(h, i, j, core).wait_send()
            mine = jnp.bool_(True) if h % 2 == 1 else j == across

            @pl.when(jnp.logical_and(mine, jnp.logical_and(i <= along, along < tall - 1)))
            def _():
                z_route(h, i, j, along + 1, up_send).wait_send()

            @pl.when(jnp.logical_and(mine, jnp.logical_and(i >= along, along > 0)))
            def _():
                z_route(h, i, j, along - 1, down_send).wait_send()

            return carry

        lax.fori_loop(0, chips, finish, 0)
        for s in range(1, wide):
            if h % 2 == 1:
                x_route(h, along, s).wait_send()
            else:
                for i in range(tall):
                    x_route(h, i, s).wait_send()
        for d in range(tall):
            for s in range(wide):
                pair_copy(h, s, d).wait_send()
                if s > 0:
                    x_copy(h, s, d).wait_send()
            if d > 0:
                z_copy(h, d).wait_send()


def exchange(parts, collective_id):
    count = lax.axis_size("seq")
    chips = count // 2
    tall = 4 if chips % 4 == 0 else chips
    wide = chips // tall
    inputs = len(parts)
    own = parts[0].shape[1] // count
    subs = 2 if inputs == 1 and own % 32 == 0 else 1
    halves = inputs * subs
    piece = own // subs
    shape = (3, 2, subs, wide, tall, piece, BLK)
    chunk = (3, piece, BLK)
    dma = pltpu.SemaphoreType.DMA
    anywhere = pl.BlockSpec(memory_space=pl.ANY)
    out = pl.pallas_call(
        functools.partial(exchange_kernel, count, inputs),
        out_shape=jax.ShapeDtypeStruct((inputs,) + shape, jnp.bfloat16),
        in_specs=[anywhere] * inputs,
        out_specs=anywhere,
        scratch_shapes=[
            pltpu.VMEM((halves, wide, tall) + chunk, jnp.float32),
            pltpu.VMEM((halves, wide, tall) + chunk, jnp.float32),
            pltpu.VMEM((halves, max(wide - 1, 1), tall) + chunk, jnp.bfloat16),
            pltpu.VMEM((halves, max(wide - 1, 1), tall) + chunk, jnp.bfloat16),
            pltpu.VMEM((halves, max(tall - 1, 1)) + chunk, jnp.bfloat16),
            pltpu.VMEM((halves, max(tall - 1, 1)) + chunk, jnp.bfloat16),
            pltpu.VMEM((halves,) + chunk, jnp.bfloat16),
            dma((halves, wide, tall)),
            dma((halves, wide, tall)),
            dma((halves, wide, tall)),
            dma((halves, wide, tall)),
            dma((halves, wide, tall)),
            dma((halves, tall)),
            dma((halves, tall)),
            dma((halves, chips)),
            dma((halves, chips)),
            dma((halves, wide, tall)),
            dma((halves, chips)),
            dma((halves, chips)),
            dma((halves, chips)),
            dma((halves,)),
        ],
        compiler_params=pltpu.CompilerParams(
            collective_id=collective_id, has_side_effects=True, vmem_limit_bytes=COMM_LIMIT
        ),
    )(*(part.reshape(shape) for part in parts))
    return out.reshape((inputs,) + parts[0].shape)


def rows_out_kernel(group, table_ref, act_ref, *refs):
    gates, ups, downs = refs[:group], refs[group : 2 * group], refs[2 * group : 3 * group]
    out_ref = refs[3 * group]
    step = pl.program_id(1)

    @pl.when(step == 0)
    def _():
        out_ref[...] = jnp.zeros_like(out_ref)

    out = jnp.zeros(out_ref.shape[2:], jnp.float32)
    grad = jnp.zeros(out_ref.shape[2:], jnp.float32)
    across = (((1,), (1,)), ((), ()))
    for at in range(group):
        rows = slice(at * ROWBLK, (at + 1) * ROWBLK)
        out += jnp.dot(act_ref[0, 0, rows, :], downs[at][...], preferred_element_type=jnp.float32)
        grad += lax.dot_general(
            jnp.concatenate([act_ref[0, 1, rows, :], act_ref[0, 2, rows, :]], axis=1),
            jnp.concatenate([gates[at][...], ups[at][...]], axis=1),
            across,
            preferred_element_type=jnp.float32,
        )
    out_ref[0, 0] += out
    out_ref[0, 1] += grad


def rows_out(table, first, row_blocks, capacity, acts, gate_w, up_w, down_w):
    feats = gate_w.shape[0]
    group = group_of(capacity)
    steps = capacity // group
    if acts.shape[0] == row_blocks:
        place = lambda row, step, table: (row, 0, step, 0)
    else:
        place = lambda row, step, table: (0, 0, row * steps + step, 0)
    flops = 6 * row_blocks * ROWBLK * feats * capacity * BLK
    return pl.pallas_call(
        functools.partial(rows_out_kernel, group),
        out_shape=jax.ShapeDtypeStruct((row_blocks, 2, ROWBLK, feats), jnp.float32),
        grid_spec=pltpu.PrefetchScalarGridSpec(
            num_scalar_prefetch=1,
            grid=(row_blocks, steps),
            in_specs=[pl.BlockSpec((1, 3, group * ROWBLK, BLK), place)]
            + weight_specs(first, group, feats),
            out_specs=pl.BlockSpec((1, 2, ROWBLK, feats), lambda row, step, table: (row, 0, 0, 0)),
        ),
        compiler_params=pltpu.CompilerParams(vmem_limit_bytes=PLAIN_LIMIT),
        cost_estimate=pl.CostEstimate(
            flops=flops, bytes_accessed=flops // ROWBLK, transcendentals=0
        ),
    )(table, acts, *([gate_w] * group + [up_w] * group + [down_w] * group))


def weights_out_kernel(first, capacity, scale, pieces, group, passing, table_ref, *refs):
    toks, cots, refs = refs[:pieces], refs[pieces : 2 * pieces], refs[2 * pieces :]
    flipped, cot_all, dense = refs[-3:]
    units, refs = refs[:-3], None
    passed = ()
    if passing:
        units, passed = units[:-2], units[-2:]
    gate_ref, up_ref, down_ref = units[-3:]
    units = units[:-3]
    step = pl.program_id(0)
    rows = flipped.shape[1]
    row_blocks = rows // ROWBLK
    each = rows // pieces

    @pl.when(step == 0)
    def _():
        for at in range(pieces):
            cut = slice(at * each, (at + 1) * each)
            flipped[:, cut] = toks[at][...].T
            cot_all[cut, :] = cots[at][...]
        for at, out in enumerate(passed):
            out[...] = units[-1][at]

    for at in range(group):
        for row in range(row_blocks):
            kept = table_ref[first + row, capacity + 1 + step * group + at] >= 0
            unit = units[at * row_blocks + row]
            for which in range(3):
                value = unit[0, which]
                dense[which, row * ROWBLK : (row + 1) * ROWBLK, at * BLK : (at + 1) * BLK] = (
                    jnp.where(kept, value, jnp.zeros_like(value))
                )
    tok = flipped[...]
    gate_ref[...] = jnp.dot(tok, dense[1], preferred_element_type=jnp.float32) * scale
    up_ref[...] = jnp.dot(tok, dense[2], preferred_element_type=jnp.float32) * scale
    down_ref[...] = (
        lax.dot_general(
            dense[0], cot_all[...], (((0,), (0,)), ((), ())), preferred_element_type=jnp.float32
        )
        * scale
    )


def weights_out(table, first, capacity, toks, cots, acts, scale, passing=None):
    blocks = table.shape[1] - capacity - 1
    feats = toks[0].shape[1]
    pieces = len(toks)
    rows = pieces * toks[0].shape[0]
    row_blocks = rows // ROWBLK
    group = wide_group(blocks)
    held = acts.shape[2] // ROWBLK
    whole = pl.BlockSpec(toks[0].shape, lambda step, table: (0, 0))
    wide = pl.BlockSpec((feats, group * BLK), lambda step, table: (0, step))
    hidden = blocks * BLK

    extra, extra_shapes, extra_in = (), (), []
    if passing is not None:
        extra = (passing,)
        extra_shapes = (jax.ShapeDtypeStruct(passing.shape[1:], passing.dtype),) * 2
        extra_in = [pl.BlockSpec(passing.shape, lambda step, table: (0, 0, 0))]

    def unit_spec(at, row):
        def place(step, table):
            unit = jnp.maximum(table[first + row, capacity + 1 + step * group + at], 0)
            unit = unit + row * capacity
            return (unit // held, 0, lax.rem(unit, held), 0)

        return pl.BlockSpec((1, 3, ROWBLK, BLK), place)

    return pl.pallas_call(
        functools.partial(
            weights_out_kernel, first, capacity, scale, pieces, group, passing is not None
        ),
        out_shape=(
            jax.ShapeDtypeStruct((feats, hidden), jnp.float32),
            jax.ShapeDtypeStruct((feats, hidden), jnp.float32),
            jax.ShapeDtypeStruct((hidden, feats), jnp.float32),
        )
        + extra_shapes,
        grid_spec=pltpu.PrefetchScalarGridSpec(
            num_scalar_prefetch=1,
            grid=(blocks // group,),
            in_specs=[whole] * (2 * pieces)
            + [unit_spec(at, row) for at in range(group) for row in range(row_blocks)]
            + extra_in,
            out_specs=(
                wide,
                wide,
                pl.BlockSpec((group * BLK, feats), lambda step, table: (step, 0)),
            )
            + (whole,) * len(extra_shapes),
            scratch_shapes=[
                pltpu.VMEM((feats, rows), jnp.bfloat16),
                pltpu.VMEM((rows, feats), jnp.bfloat16),
                pltpu.VMEM((3, rows, group * BLK), jnp.bfloat16),
            ],
        ),
        compiler_params=pltpu.CompilerParams(vmem_limit_bytes=WIDE_LIMIT),
        cost_estimate=pl.CostEstimate(
            flops=6 * rows * feats * hidden, bytes_accessed=12 * feats * hidden, transcendentals=0
        ),
    )(table, *toks, *cots, *([acts] * (group * row_blocks)), *extra)


def fused_kernel(mode, count, *refs):
    swapped, both = mode == "other", mode == "both"
    rows_held = 2 if both else 1
    moving = swapped or both
    table_ref, tok_ref, cot_ref, gate_hbm, up_hbm, down_hbm = refs[:6]
    refs = refs[6:]
    acts_out, tok_out, cot_out = refs[:3] if moving else (refs[0], None, None)
    refs = refs[3 if moving else 1 :]
    outs, refs = refs[:rows_held], refs[rows_held:]
    (
        gate_w, up_w, down_w, toks, cots, parts, paired, xsend, xland, zsend, zland, acts,
        sums, weight_sem, row_load, row_send, row_recv, row_store, pair_send, pair_recv, x_send, x_recv,
        z_send, z_recv, up_send, down_send, side_send, all_recv, hand_send, hand_recv, out_sem,
    ) = refs
    groups, _, held, _ = parts.shape
    rows = toks.shape[0]
    first = 1 if swapped else 0
    units = held // ROWBLK
    _, wide, tall, _, piece, _ = paired.shape
    chips = count // 2
    me, rank = lax.axis_index("seq"), lax.axis_index("tp")
    chip, core = me // 2, lax.rem(me, 2)
    sibling, partner = {"seq": me + 1 - 2 * core}, {"tp": 1 - rank}
    along, across = chip // wide, lax.rem(chip, wide)
    order = sorted(range(1, tall), key=lambda shift: abs(2 * shift - tall))
    contract = (((1,), (1,)), ((), ()))

    def device(i, j):
        return {"seq": (i * wide + j) * 2 + core}

    def column(shift):
        return lax.rem(across + shift, wide)

    def line(shift):
        return lax.rem(along + shift, tall)

    def rows_of(side, i, j):
        return pl.ds(pl.multiple_of(((side * wide + j) * tall + i) * piece, 16), piece)

    def remote(src, dst, send, recv, target):
        return pltpu.make_async_remote_copy(
            src_ref=src, dst_ref=dst, send_sem=send, recv_sem=recv,
            device_id=target, device_id_type=MESH,
        )

    def signal(target):
        pl.semaphore_signal(
            pltpu.get_barrier_semaphore(), inc=1, device_id=target, device_id_type=MESH
        )

    blocks = down_w.shape[0]
    own_rows = [
        pltpu.make_async_copy(src, dst.at[0], row_load.at[at])
        for at, (src, dst) in enumerate(((tok_ref, toks), (cot_ref, cots)))
        if not swapped
    ]

    def start_columns(block, carry):
        cut = pl.ds(pl.multiple_of(block * BLK, BLK), BLK)
        pltpu.make_async_copy(gate_hbm.at[:, cut], gate_w.at[block], weight_sem.at[0]).start()
        pltpu.make_async_copy(up_hbm.at[:, cut], up_w.at[block], weight_sem.at[1]).start()
        return carry

    def start_lines(block, carry):
        cut = pl.ds(pl.multiple_of(block * BLK, BLK), BLK)
        pltpu.make_async_copy(down_hbm.at[cut, :], down_w.at[block], weight_sem.at[2]).start()
        return carry

    for copy in own_rows:
        copy.start()
    lax.fori_loop(0, blocks, start_columns, 0)
    lax.fori_loop(0, blocks, start_lines, 0)

    signal(sibling)
    for s in range(1, wide):
        signal(device(along, column(s)))
    for d in range(1, tall):
        signal(device(line(d), across))
    if moving:
        signal(partner)
    pl.semaphore_wait(pltpu.get_barrier_semaphore(), wide + tall - 1 + (1 if moving else 0))

    row_copies = [
        remote(src, dst.at[rows - 1], row_send.at[at], row_recv.at[at], partner)
        for at, (src, dst) in enumerate(((tok_ref, toks), (cot_ref, cots)))
        if moving
    ]
    for copy in row_copies:
        copy.start()
    row_stores = [
        pltpu.make_async_copy(src.at[rows - 1], dst, row_store.at[at])
        for at, (src, dst) in enumerate(((toks, tok_out), (cots, cot_out)))
        if moving
    ]

    def pair_copy(h, s, d):
        return remote(
            parts.at[h, :, rows_of(1 - core, line(d), column(s))], paired.at[h, s, d],
            pair_send.at[h, s, d], pair_recv.at[h, s, d], sibling,
        )

    def x_copy(h, s, d):
        return remote(
            xsend.at[h, s - 1, d], xland.at[h, s - 1, d],
            x_send.at[h, s, d], x_recv.at[h, s, d], device(along, column(s)),
        )

    def z_copy(h, d):
        return remote(
            zsend.at[h, d - 1], zland.at[h, d - 1],
            z_send.at[h, d], z_recv.at[h, d], device(line(d), across),
        )

    def slot(h, i, j, side):
        return acts.at[h, :, rows_of(side, i, j)]

    def z_route(h, i, j, to, send):
        dst, owner = slot(h, i, j, core), i * wide + j
        return remote(
            dst, dst, send.at[h, owner], all_recv.at[h, owner], device(to, across)
        )

    def x_route(h, i, s):
        dst = slot(h, i, across, core)
        return remote(
            dst, dst, side_send.at[h, s, i], all_recv.at[h, i * wide + across],
            device(along, column(s)),
        )

    def hand_copy(h, i, j, side):
        dst, owner = slot(h, i, j, side), i * wide + j
        return remote(dst, dst, hand_send.at[h, owner], hand_recv.at[h, owner], sibling)

    def out_copy(h):
        return pltpu.make_async_copy(acts.at[h], acts_out.at[h], out_sem.at[h])

    def take(h, i, j):
        z_route(h, i, j, along, up_send).wait_recv()

    def pass_on(h, i, j, up, down):
        if up:

            @pl.when(along < tall - 1)
            def _():
                z_route(h, i, j, along + 1, up_send).start()

        if down:

            @pl.when(along > 0)
            def _():
                z_route(h, i, j, along - 1, down_send).start()

    def spread(h, i):
        for s in range(1, wide):
            x_route(h, i, s).start()

    def line_first(h):
        return True

    def row_of(h):
        return h * rows // groups

    def block_of(h, unit):
        base = h % (groups // rows) * units
        return table_ref[first + row_of(h), base + unit]

    def unit_rows(unit):
        return pl.ds(pl.multiple_of(unit * ROWBLK, ROWBLK), ROWBLK)

    begin = (1 - core) * (units // 2 // 2)

    def column_step(h, pair):
        tok = toks[row_of(h)]
        for one in range(2):
            block, at = block_of(h, 2 * pair + one), unit_rows(2 * pair + one)
            value = jnp.dot(
                tok,
                jnp.concatenate([gate_w[block], up_w[block]], axis=1),
                preferred_element_type=jnp.float32,
            )
            parts[h, 0, at, :] = value[:, :BLK]
            parts[h, 1, at, :] = value[:, BLK:]

    def line_step(h, pair):
        grad = lax.dot_general(
            cots[row_of(h)],
            jnp.concatenate(
                [down_w[block_of(h, 2 * pair)], down_w[block_of(h, 2 * pair + 1)]], axis=0
            ),
            contract,
            preferred_element_type=jnp.float32,
        )
        parts[h, 2, unit_rows(2 * pair), :] = grad[:, :BLK]
        parts[h, 2, unit_rows(2 * pair + 1), :] = grad[:, BLK:]

    def each_pair(h, low, high, *steps):
        def body(turn, carry):
            for step in steps:
                step(h, lax.rem(turn + begin, units // 2))
            return carry

        lax.fori_loop(low, high, body, 0)

    def columns_times(h, low, high):
        each_pair(h, low, high, column_step)

    def lines_times(h, low, high):
        each_pair(h, low, high, line_step)

    def multiply(h, low, high):
        each_pair(h, low, high, column_step, line_step)

    def pair_stage(h):
        for s in list(range(1, wide)) + [0]:
            for d in order + [0]:
                pair_copy(h, s, d).start()

    def x_stage(h):
        for d in order + [0]:
            for s in range(1, wide):
                pair_copy(h, s, d).wait_recv()
                xsend[h, s - 1, d] = (
                    parts[h, :, rows_of(core, line(d), column(s)), :] + paired[h, s, d]
                ).astype(jnp.bfloat16)
                x_copy(h, s, d).start()

    def row_sum(h, d):
        pair_copy(h, 0, d).wait_recv()
        total = parts[h, :, rows_of(core, line(d), across), :] + paired[h, 0, d]
        for s in range(1, wide):
            x_copy(h, s, d).wait_recv()
            total = total + xland[h, s - 1, d].astype(jnp.float32)
        return total

    def z_piece(h, at):
        d = order[at]
        zsend[h, d - 1] = row_sum(h, d).astype(jnp.bfloat16)
        z_copy(h, d).start()

    def z_stage(h):
        for at in range(len(order)):
            z_piece(h, at)

    def act_stage(h):
        total = row_sum(h, 0)
        for d in order:
            z_copy(h, d).wait_recv()
            total = total + zland[h, d - 1].astype(jnp.float32)
        gate, up, grad = total[0], total[1], total[2]
        sig = jax.nn.sigmoid(gate)
        own = rows_of(core, along, across)
        acts[h, 0, own, :] = (gate * sig * up).astype(jnp.bfloat16)
        acts[h, 1, own, :] = (grad * up * sig * (1.0 + gate * (1.0 - sig))).astype(jnp.bfloat16)
        acts[h, 2, own, :] = (grad * gate * sig).astype(jnp.bfloat16)
        pass_on(h, along, across, True, True)
        spread(h, along)
        hand_copy(h, along, across, core).start()

    def gather_stage(h, far):
        if far == 1 and not line_first(h):
            for s in range(1, wide):
                take(h, along, column(s))
                pass_on(h, along, column(s), True, True)
                hand_copy(h, along, column(s), core).start()
        for s in range(1 if line_first(h) else wide):
            for sign in (-1, 1):

                @pl.when(along >= far if sign < 0 else along + far < tall)
                def _(s=s, sign=sign):
                    i = along + sign * far
                    take(h, i, column(s))
                    pass_on(h, i, column(s), sign < 0, sign > 0)
                    if line_first(h):
                        spread(h, i)
                    hand_copy(h, i, column(s), core).start()

    def side_stage(h):
        if line_first(h):
            for s in range(1, wide):
                for d in range(tall):
                    take(h, line(d), column(s))
                    hand_copy(h, line(d), column(s), core).start()

    def sums_stage(h):
        def arrive(owner, carry):
            hand_copy(h, owner // wide, lax.rem(owner, wide), 1 - core).wait_recv()
            return carry

        lax.fori_loop(0, chips, arrive, 0)
        out_copy(h).start()
        row = row_of(h)

        def step(pair, carry):
            at = (unit_rows(2 * pair), unit_rows(2 * pair + 1))
            cut = (block_of(h, 2 * pair), block_of(h, 2 * pair + 1))
            sums[row, 0] += jnp.dot(
                jnp.concatenate([acts[h, 0, at[0], :], acts[h, 0, at[1], :]], axis=1),
                jnp.concatenate([down_w[cut[0]], down_w[cut[1]]], axis=0),
                preferred_element_type=jnp.float32,
            )
            grad = sums[row, 1]
            for one in range(2):
                grad += lax.dot_general(
                    jnp.concatenate([acts[h, 1, at[one], :], acts[h, 2, at[one], :]], axis=1),
                    jnp.concatenate([gate_w[cut[one]], up_w[cut[one]]], axis=1),
                    contract,
                    preferred_element_type=jnp.float32,
                )
            sums[row, 1] = grad
            return carry

        lax.fori_loop(0, units // 2, step, 0)

    sums[...] = jnp.zeros_like(sums)
    for copy in own_rows:
        copy.wait()
    half = (units // 2 + 1) // 2

    def weights_arrive(at, held_w):
        pltpu.make_async_copy(held_w, held_w, weight_sem.at[at]).wait()

    pairs = units // 2
    early = groups > 2
    for h in range(groups):
        crossing = moving and h == (0 if swapped else groups // 2)
        if h == 0:
            weights_arrive(0, gate_w)
            weights_arrive(1, up_w)
        if crossing:
            row_copies[0].wait_recv()
        columns_times(h, 0, half)
        if h == 0:
            weights_arrive(2, down_w)
        if crossing:
            row_copies[1].wait_recv()
            for copy in row_stores:
                copy.start()
        lines_times(h, 0, half)
        pair_stage(h)
        multiply(h, half, pairs)
        if h > 0:
            for at in range(len(order) - 1):
                z_piece(h - 1, at)
        x_stage(h)
        if h > 0:
            z_piece(h - 1, len(order) - 1)
        if early and h == groups - 1:
            act_stage(0)
    last = tall + 1
    for turn in range(groups + last):
        if turn == groups - 2:
            z_stage(groups - 1)
        for h in range(groups):
            at = turn - h
            if 1 <= at < tall:
                gather_stage(h, at)
            elif at == tall:
                side_stage(h)
            elif at == 0 and not (early and h == 0):
                act_stage(h)
        if 0 <= turn - last < groups:
            sums_stage(turn - last)

    alive = table_ref[first + rows - 1, table_ref.shape[1] - 1].astype(jnp.float32)
    for row, out in enumerate(outs):
        value = sums[row]
        if both:
            value = value * alive
        out[...] = value.astype(out.dtype)

    for h in range(groups):

        def finish(owner, carry, h=h):
            i, j = owner // wide, lax.rem(owner, wide)
            hand_copy(h, i, j, core).wait_send()
            mine = j == across if line_first(h) else jnp.bool_(True)

            @pl.when(jnp.logical_and(mine, jnp.logical_and(i <= along, along < tall - 1)))
            def _():
                z_route(h, i, j, along + 1, up_send).wait_send()

            @pl.when(jnp.logical_and(mine, jnp.logical_and(i >= along, along > 0)))
            def _():
                z_route(h, i, j, along - 1, down_send).wait_send()

            return carry

        lax.fori_loop(0, chips, finish, 0)
        for s in range(1, wide):
            if line_first(h):
                for i in range(tall):
                    x_route(h, i, s).wait_send()
            else:
                x_route(h, along, s).wait_send()
        for d in range(tall):
            for s in range(wide):
                pair_copy(h, s, d).wait_send()
                if s > 0:
                    x_copy(h, s, d).wait_send()
            if d > 0:
                z_copy(h, d).wait_send()
        out_copy(h).wait()
    for copy in row_copies:
        copy.wait_send()
    for copy in row_stores:
        copy.wait()


def fused(mode, table, capacity, tok, cot, gate_w, up_w, down_w, collective_id):
    count = lax.axis_size("seq")
    chips = count // 2
    tall = 4 if chips % 4 == 0 else chips
    wide = chips // tall
    rows = 2 if mode == "both" else 1
    groups = 2 * rows
    feats, blocks = gate_w.shape[0], gate_w.shape[1] // BLK
    held = capacity // 2 * ROWBLK
    piece = held // count
    chunk = (3, piece, BLK)
    dma = pltpu.SemaphoreType.DMA
    anywhere = pl.BlockSpec(memory_space=pl.ANY)
    out_shape = [jax.ShapeDtypeStruct((groups, 3, held, BLK), jnp.bfloat16)]
    out_specs = [anywhere]
    if mode != "own":
        out_shape += [jax.ShapeDtypeStruct(tok.shape, tok.dtype)] * 2
        out_specs += [anywhere] * 2
    if mode == "both":
        out_shape += [jax.ShapeDtypeStruct((2,) + tok.shape, jnp.float32)]
    out_shape += [jax.ShapeDtypeStruct((2,) + tok.shape, jnp.bfloat16)]
    out_specs += [pl.BlockSpec(memory_space=pltpu.VMEM)] * rows
    flops = 12 * rows * ROWBLK * tok.shape[1] * capacity * BLK
    return pl.pallas_call(
        functools.partial(fused_kernel, mode, count),
        out_shape=tuple(out_shape),
        in_specs=[pl.BlockSpec(memory_space=pltpu.SMEM)] + [anywhere] * 5,
        out_specs=tuple(out_specs),
        scratch_shapes=[
            pltpu.VMEM((blocks, feats, BLK), gate_w.dtype),
            pltpu.VMEM((blocks, feats, BLK), up_w.dtype),
            pltpu.VMEM((blocks, BLK, feats), down_w.dtype),
            pltpu.VMEM((rows,) + tok.shape, tok.dtype),
            pltpu.VMEM((rows,) + tok.shape, tok.dtype),
            pltpu.VMEM((groups, 3, held, BLK), jnp.float32),
            pltpu.VMEM((groups, wide, tall) + chunk, jnp.float32),
            pltpu.VMEM((groups, wide - 1, tall) + chunk, jnp.bfloat16),
            pltpu.VMEM((groups, wide - 1, tall) + chunk, jnp.bfloat16),
            pltpu.VMEM((groups, tall - 1) + chunk, jnp.bfloat16),
            pltpu.VMEM((groups, tall - 1) + chunk, jnp.bfloat16),
            pltpu.VMEM((groups, 3, held, BLK), jnp.bfloat16),
            pltpu.VMEM((rows, 2) + tok.shape, jnp.float32),
            dma((3,)),
            dma((2,)),
            dma((2,)),
            dma((2,)),
            dma((2,)),
            dma((groups, wide, tall)),
            dma((groups, wide, tall)),
            dma((groups, wide, tall)),
            dma((groups, wide, tall)),
            dma((groups, tall)),
            dma((groups, tall)),
            dma((groups, chips)),
            dma((groups, chips)),
            dma((groups, wide, tall)),
            dma((groups, chips)),
            dma((groups, chips)),
            dma((groups, chips)),
            dma((groups,)),
        ],
        compiler_params=pltpu.CompilerParams(
            collective_id=collective_id, has_side_effects=True, vmem_limit_bytes=FUSED_LIMIT
        ),
        cost_estimate=pl.CostEstimate(
            flops=flops, bytes_accessed=6 * gate_w.size, transcendentals=0
        ),
    )(table, tok, cot, gate_w, up_w, down_w)


def shards(tokens, gate_weight, up_weight, down_weight, masks, cotangent):
    tp_count = lax.axis_size("tp")
    seq_count = lax.axis_size("seq")
    rank = lax.axis_index("tp")
    rows, feats = tokens.shape
    total_rows = rows * tp_count
    row_blocks, blocks = masks.shape
    kept_total = blocks * tp_count // KEEP_PART
    capacity = min(2 * kept_total // tp_count, blocks)
    scale = 1.0 / math.sqrt(total_rows)
    weights = (gate_weight, up_weight, down_weight)

    fits = seq_count % 8 == 0 and capacity % 4 == 0 and capacity // 2 * ROWBLK % (16 * seq_count) == 0
    if tp_count != 2 or row_blocks != 2 or rows != ROWBLK or not fits:
        table, _, _ = unit_tables(masks, jnp.int32(0), capacity)
        tok, cot = (value.reshape(total_rows, feats) for value in gather_rows(tokens, cotangent))
        parts = partial_products(table, 0, capacity, tok, cot, *weights)
        acts = exchange([parts], 1)
        row_parts = rows_out(table, 0, row_blocks, capacity, acts, *weights)
        row_parts = jnp.swapaxes(row_parts.reshape(tp_count, rows // ROWBLK, 2, ROWBLK, feats), 1, 2)
        moved = []
        for shift in range(1, tp_count):
            piece = lax.dynamic_index_in_dim(
                row_parts, lax.rem(rank + shift, tp_count), 0, keepdims=False
            ).astype(jnp.bfloat16)
            pairs = [(src, (src + shift) % tp_count) for src in range(tp_count)]
            moved.append(lax.ppermute(piece, "tp", pairs))
        grads = weights_out(table, 0, capacity, [tok], [cot], acts, scale)
        mine = lax.dynamic_index_in_dim(row_parts, rank, 0, keepdims=False)
        for piece in moved:
            mine = mine + piece.astype(jnp.float32)
        mine = mine.reshape(2, rows, feats).astype(jnp.bfloat16)
        return (mine[0], mine[1]) + tuple(grads)

    table, index, case = unit_tables(masks, rank, capacity)

    def swap(value):
        return lax.ppermute(value, "tp", [(0, 1), (1, 0)])

    def one_row(own, _):
        first = 0 if own else 1
        acts, *rest = fused(
            "own" if own else "other", index, capacity, tokens, cotangent, *weights, 2 + first
        )
        if own:
            grads = weights_out(table, 0, capacity, [tokens], [cotangent], acts, scale, rest[0])
            return tuple(grads[3:]) + tuple(grads[:3])
        tok, cot, sums = rest
        sums = swap(sums)
        grads = weights_out(table, 1, capacity, [tok], [cot], acts, scale)
        return (sums[0], sums[1]) + tuple(grads)

    def both_rows(_):
        acts, tok, cot, mine, other = fused(
            "both", index, capacity, tokens, cotangent, *weights, 1
        )
        moved = swap(other)
        grads = weights_out(table, 0, capacity, [tokens, tok], [cotangent, cot], acts, scale)
        total = (mine + moved.astype(jnp.float32)).astype(jnp.bfloat16)
        return (total[0], total[1]) + tuple(grads)

    return lax.switch(
        case[0],
        [functools.partial(one_row, True), functools.partial(one_row, False), both_rows],
        None,
    )


def solution(mesh):
    placed = (
        P("tp", "seq"),
        P("seq", "tp"),
        P("seq", "tp"),
        P("tp", "seq"),
        P(None, "tp"),
        P("tp", "seq"),
    )
    return jax.shard_map(
        shards,
        mesh=mesh,
        in_specs=placed,
        out_specs=(P("tp", "seq"), P("tp", "seq"), P("seq", "tp"), P("seq", "tp"), P("tp", "seq")),
        check_vma=False,
    )
```

profile of v0, /device:TPU:0, one launch (start us, length us, event | category | flops | bytes accessed | tf_op | source)
XLA Modules:
  0.0 113.6 jit_solution(14238568097646370750)
XLA Ops:
  0.6 2.2 %shard_map.101 = (s32[2,85]{1,0:T(2,128)S(1)}, s32[2,29]{1,0:T(2,128)S(1)}, s32[1]{0:T(128)}) custom-call(s32[1]{0:T(128)} %bitcast.4.first_ref, s32[2,56]{1,0:T(2,128)} %mask_ref.1), custom_call_target="tpu_custom_call" | custom-call | tf_op jit(solution)/shard_map/pallas_call | solution.py:68
  3.5 110.1 %conditional.1 = (bf16[128,512]{1,0:T(8,128)(2,1)}, bf16[128,512]{1,0:T(8,128)(2,1)}, f32[512,7168]{1,0:T(8,128)}, f32[512,7168]{1,0:T(8,128)}, f32[7168,512]{1,0:T(8,128)}) conditional(s32[]{:T(128)} %bitcast.5, (s32[2,29]{1,0:T(2,128)S(1)}, bf16[128,512]{1,0:T(8,128)(2,1)}, bf16[128,512]{1,0:T(8,128)(2,1)}, ...), branch_computations={%region_0.0_spmd, %region_1.0_spmd, %region_2.0_spmd} | conditional | flops 11274682368 | bytes 71827624 | solution.py:1151
  3.7 0.0 copy-start.1
  3.7 0.0 copy-start.3
  3.7 87.6 %branch_2_fun.2 = (bf16[4,3,1792,128]{3,2,1,0:T(8,128)(2,1)}, bf16[128,512]{1,0:T(8,128)(2,1)}, bf16[128,512]{1,0:T(8,128)(2,1)}, f32[2,128,512]{2,1,0:T(8,128)}, bf16[2,128,512]{2,1,0:T(8,128)(2,1)}) custom-call(s32[2,29]{1,0:T(2,128)S(1)} %get-tuple-element.70.refs_0_, bf16[128,512]{1,0:T(8,128)(2,1)} %get-tuple-element.71.refs_1_.refs_0_, ...), custom_call_target="tpu_custom_call" | custom-call | flops 5637144576 | bytes 22020096 | tf_op jit(solution)/shard_map/cond/branch_2_fun/pallas_call | solution.py:1043
  91.3 1.6 %collective-permute-start.1 = (bf16[2,128,512]{2,1,0:T(8,128)(2,1)}, bf16[2,128,512]{2,1,0:T(8,128)(2,1)S(1)}, u32[]{:S(2)}, u32[]{:S(2)}) collective-permute-start(bf16[2,128,512]{2,1,0:T(8,128)(2,1)} %get-tuple-element.77), channel_id=1, source_target_pairs={{0,1},{1,0},{2,3},{3,2},{4,5},{5,4},{6,7},{7,6},{8,9},{9,8},{10,11... | collective-permute-start | bytes 786440 | tf_op jit(solution)/shard_map/cond/branch_2_fun/ppermute | solution.py:1127
  92.9 0.0 copy-done.1
  92.9 0.0 copy-done.3
  92.9 0.0 copy-start.4
  92.9 19.8 %branch_2_fun.3 = (f32[512,7168]{1,0:T(8,128)}, f32[512,7168]{1,0:T(8,128)}, f32[7168,512]{1,0:T(8,128)}) custom-call(s32[2,85]{1,0:T(2,128)S(1)} %get-tuple-element.78.table_ref, bf16[128,512]{1,0:T(8,128)(2,1)S(1)} %copy-done.1, bf16[128,512]{1,0:T(8,128)(2,1)} %get-tuple-element.79.refs_1_, bf16[128,512]{1,0:T(8,128)(2,1)S(1)} %copy-done.3, ...), custom_call_target="tpu_custom_call" | custom-call | flops 5637144576 | bytes 44040192 | tf_op jit(solution)/shard_map/cond/branch_2_fun/pallas_call | solution.py:577
  112.7 0.0 collective-permute-done.1
  112.7 0.0 copy-done.4
  112.8 0.1 add_convert_fusion
  112.8 0.7 slice_bitcast_fusion.2
Async XLA Ops:
  3.7 89.2 %copy-start.1 = (bf16[128,512]{1,0:T(8,128)(2,1)S(1)}, bf16[128,512]{1,0:T(8,128)(2,1)}, u32[]{:S(2)}) copy-start(bf16[128,512]{1,0:T(8,128)(2,1)} %get-tuple-element.71.refs_1_.refs_0_) | copy-start | bytes 393220 | tf_op jit(solution)/shard_map/cond
  3.7 89.2 %copy-start.3 = (bf16[128,512]{1,0:T(8,128)(2,1)S(1)}, bf16[128,512]{1,0:T(8,128)(2,1)}, u32[]{:S(2)}) copy-start(bf16[128,512]{1,0:T(8,128)(2,1)} %get-tuple-element.72.refs_2_) | copy-start | bytes 393220 | tf_op jit(solution)/shard_map/cond
  91.3 21.4 %collective-permute-start.1 = (bf16[2,128,512]{2,1,0:T(8,128)(2,1)}, bf16[2,128,512]{2,1,0:T(8,128)(2,1)S(1)}, u32[]{:S(2)}, u32[]{:S(2)}) collective-permute-start(bf16[2,128,512]{2,1,0:T(8,128)(2,1)} %get-tuple-element.77), channel_id=1, source_target_pairs={{0,1},{1,0},{2,3},{3,2},{4,5},{5,4},{6,7},{7,6},{8,9},{9,8},{10,11... | collective-permute-start | bytes 786440 | tf_op jit(solution)/shard_map/cond/branch_2_fun/ppermute | solution.py:1127
  92.9 19.8 %copy-start.4 = (f32[2,128,512]{2,1,0:T(8,128)S(1)}, f32[2,128,512]{2,1,0:T(8,128)}, u32[]{:S(2)}) copy-start(f32[2,128,512]{2,1,0:T(8,128)} %get-tuple-element.76) | copy-start | bytes 1572868 | tf_op jit(solution)/shard_map/cond
where the time goes:
time: 113 us; the launch traced here: 114 us
  Pallas kernels  110 us (97%)
  starting transfers between devices  1.58 us (1%)
  between operations  1.29 us (1%)
    pallas_call x1, Pallas kernels, fused(): pl.pallas_call(functools.partial(fused_kernel, mode, count), out_shape=tu...  87.6 us
    pallas_call x1, Pallas kernels, weights_out(): pl.pallas_call(functools.partial(weights_out_kernel, first, capacity, sca...  19.8 us
  transfers between devices with their start and end apart: 1, of which 0 were waited for; matrix products, arithmetic and copies ran while one was open for 0% of the time, Pallas kernels for 17%

commit v1 on v0

--- a/solution.py
+++ b/solution.py
@@ -14,7 +14,7 @@
 MESH = pl.DeviceIdType.MESH
 PLAIN_LIMIT = 20 * 1024 * 1024
 COMM_LIMIT = 28 * 1024 * 1024
-WIDE_LIMIT = 60 * 1024 * 1024
+WIDE_LIMIT = 32 * 1024 * 1024
 FUSED_LIMIT = 60 * 1024 * 1024
 
 
@@ -528,14 +528,18 @@
         for at, out in enumerate(passed):
             out[...] = units[-1][at]
 
+    act_ref = units[0]
+    held = act_ref.shape[2] // ROWBLK
     for at in range(group):
         for row in range(row_blocks):
-            kept = table_ref[first + row, capacity + 1 + step * group + at] >= 0
-            unit = units[at * row_blocks + row]
+            unit = table_ref[first + row, capacity + 1 + step * group + at]
+            index = jnp.maximum(unit, 0) + row * capacity
+            lead, index = index // held, lax.rem(index, held)
+            taken = pl.ds(pl.multiple_of(index * ROWBLK, ROWBLK), ROWBLK)
             for which in range(3):
-                value = unit[0, which]
+                value = act_ref[lead, which, taken, :]
                 dense[which, row * ROWBLK : (row + 1) * ROWBLK, at * BLK : (at + 1) * BLK] = (
-                    jnp.where(kept, value, jnp.zeros_like(value))
+                    jnp.where(unit >= 0, value, jnp.zeros_like(value))
                 )
     tok = flipped[...]
     gate_ref[...] = jnp.dot(tok, dense[1], preferred_element_type=jnp.float32) * scale
@@ -553,9 +557,7 @@
     feats = toks[0].shape[1]
     pieces = len(toks)
     rows = pieces * toks[0].shape[0]
-    row_blocks = rows // ROWBLK
     group = wide_group(blocks)
-    held = acts.shape[2] // ROWBLK
     whole = pl.BlockSpec(toks[0].shape, lambda step, table: (0, 0))
     wide = pl.BlockSpec((feats, group * BLK), lambda step, table: (0, step))
     hidden = blocks * BLK
@@ -565,14 +567,6 @@
         extra = (passing,)
         extra_shapes = (jax.ShapeDtypeStruct(passing.shape[1:], passing.dtype),) * 2
         extra_in = [pl.BlockSpec(passing.shape, lambda step, table: (0, 0, 0))]
-
-    def unit_spec(at, row):
-        def place(step, table):
-            unit = jnp.maximum(table[first + row, capacity + 1 + step * group + at], 0)
-            unit = unit + row * capacity
-            return (unit // held, 0, lax.rem(unit, held), 0)
-
-        return pl.BlockSpec((1, 3, ROWBLK, BLK), place)
 
     return pl.pallas_call(
         functools.partial(
@@ -588,7 +582,7 @@
             num_scalar_prefetch=1,
             grid=(blocks // group,),
             in_specs=[whole] * (2 * pieces)
-            + [unit_spec(at, row) for at in range(group) for row in range(row_blocks)]
+            + [pl.BlockSpec(acts.shape, lambda step, table: (0, 0, 0, 0))]
             + extra_in,
             out_specs=(
                 wide,
@@ -606,7 +600,7 @@
         cost_estimate=pl.CostEstimate(
             flops=6 * rows * feats * hidden, bytes_accessed=12 * feats * hidden, transcendentals=0
         ),
-    )(table, *toks, *cots, *([acts] * (group * row_blocks)), *extra)
+    )(table, *toks, *cots, acts, *extra)
 
 
 def fused_kernel(mode, count, *refs):
@@ -961,6 +955,8 @@
     for turn in range(groups + last):
         if turn == groups - 2:
             z_stage(groups - 1)
+        if 0 <= turn - last < groups:
+            sums_stage(turn - last)
         for h in range(groups):
             at = turn - h
             if 1 <= at < tall:
@@ -969,8 +965,6 @@
                 side_stage(h)
             elif at == 0 and not (early and h == 0):
                 act_stage(h)
-        if 0 <= turn - last < groups:
-            sums_stage(turn - last)
 
     alive = table_ref[first + rows - 1, table_ref.shape[1] - 1].astype(jnp.float32)
     for row, out in enumerate(outs):

time: 113 us -> 112 us (level)
  Pallas kernels: 110 us -> 104 us
  local copies, waits for them, and re-layouts: 0.73 us -> 5.1 us
    cond x6 -> x12, local copies, waits for them, and re-layouts: 0.02 us -> 4.39 us
    pallas_call x1, Pallas kernels: 19.8 us -> 15.6 us  [weights_out(): pl.pallas_call(functools.partial(weights_out_kernel, first, capacity, sca...]
    pallas_call x1, Pallas kernels: 87.6 us -> 86 us  [fused(): pl.pallas_call(functools.partial(fused_kernel, mode, count), out_shape=tu...]
  transfers between devices with their start and end apart: 1 -> 1, of which waited for: 0 -> 0; matrix products, arithmetic and copies ran while one was open for 0% -> 0% of each run, Pallas kernels for 17% -> 14%
where the time goes in v1:
time: 112 us
  Pallas kernels  104 us (93%)
  local copies, waits for them, and re-layouts  5.1 us (5%)
  starting transfers between devices  1.58 us (1%)
  between operations  1.29 us (1%)
    pallas_call x1, Pallas kernels, fused(): pl.pallas_call(functools.partial(fused_kernel, mode, count), out_shape=tu...  86 us
    pallas_call x1, Pallas kernels, weights_out(): pl.pallas_call(functools.partial(weights_out_kernel, first, capacity, sca...  15.6 us
    cond x12, local copies, waits for them, and re-layouts  4.39 us
  transfers between devices with their start and end apart: 1, of which 0 were waited for; matrix products, arithmetic and copies ran while one was open for 0% of the time, Pallas kernels for 14%

profile of v1, /device:TPU:0, one launch (start us, length us, event | category | flops | bytes accessed | tf_op | source)
XLA Modules:
  0.0 112.0 jit_solution(4954966691661455454)
XLA Ops:
  0.6 2.2 %shard_map.101 = (s32[2,85]{1,0:T(2,128)S(1)}, s32[2,29]{1,0:T(2,128)S(1)}, s32[1]{0:T(128)}) custom-call(s32[1]{0:T(128)} %bitcast.4.first_ref, s32[2,56]{1,0:T(2,128)} %mask_ref.1), custom_call_target="tpu_custom_call" | custom-call | tf_op jit(solution)/shard_map/pallas_call | solution.py:68
  3.5 108.5 %conditional.1 = (bf16[128,512]{1,0:T(8,128)(2,1)}, bf16[128,512]{1,0:T(8,128)(2,1)}, f32[512,7168]{1,0:T(8,128)}, f32[512,7168]{1,0:T(8,128)}, f32[7168,512]{1,0:T(8,128)}) conditional(s32[]{:T(128)} %bitcast.5, (s32[2,29]{1,0:T(2,128)S(1)}, bf16[128,512]{1,0:T(8,128)(2,1)}, bf16[128,512]{1,0:T(8,128)(2,1)}, ...), branch_computations={%region_0.0_spmd, %region_1.0_spmd, %region_2.0_spmd} | conditional | flops 11274682368 | bytes 94896376 | solution.py:1145
  3.5 0.0 copy-start.9
  3.5 0.0 copy-start.11
  3.5 86.0 %branch_2_fun.2 = (bf16[4,3,1792,128]{3,2,1,0:T(8,128)(2,1)}, bf16[128,512]{1,0:T(8,128)(2,1)}, bf16[128,512]{1,0:T(8,128)(2,1)}, f32[2,128,512]{2,1,0:T(8,128)}, bf16[2,128,512]{2,1,0:T(8,128)(2,1)}) custom-call(s32[2,29]{1,0:T(2,128)S(1)} %get-tuple-element.70.refs_0_, bf16[128,512]{1,0:T(8,128)(2,1)} %get-tuple-element.71.refs_1_.refs_0_, ...), custom_call_target="tpu_custom_call" | custom-call | flops 5637144576 | bytes 22020096 | tf_op jit(solution)/shard_map/cond/branch_2_fun/pallas_call | solution.py:1037
  89.6 1.6 %collective-permute-start.1 = (bf16[2,128,512]{2,1,0:T(8,128)(2,1)}, bf16[2,128,512]{2,1,0:T(8,128)(2,1)S(1)}, u32[]{:S(2)}, u32[]{:S(2)}) collective-permute-start(bf16[2,128,512]{2,1,0:T(8,128)(2,1)} %get-tuple-element.77), channel_id=1, source_target_pairs={{0,1},{1,0},{2,3},{3,2},{4,5},{5,4},{6,7},{7,6},{8,9},{9,8},{10,11... | collective-permute-start | bytes 786440 | tf_op jit(solution)/shard_map/cond/branch_2_fun/ppermute | solution.py:1121
  91.2 0.0 copy-done.9
  91.2 0.0 copy-done.11
  91.2 0.0 copy-start
  91.2 2.6 %copy-done = bf16[4,3,1792,128]{3,2,1,0:T(8,128)(2,1)S(1)} copy-done((bf16[4,3,1792,128]{3,2,1,0:T(8,128)(2,1)S(1)}, bf16[4,3,1792,128]{3,2,1,0:T(8,128)(2,1)}, u32[]{:S(2)}) %copy-start) | copy-done | bytes 5505048 | tf_op jit(solution)/shard_map/cond
  93.7 0.0 copy-start.4
  93.7 0.9 copy-done.4
  94.6 0.0 copy-start.5
  94.6 0.9 copy-done.5
  95.5 0.0 copy-start.12
  95.5 15.6 %branch_2_fun.3 = (f32[512,7168]{1,0:T(8,128)}, f32[512,7168]{1,0:T(8,128)}, f32[7168,512]{1,0:T(8,128)}) custom-call(s32[2,85]{1,0:T(2,128)S(1)} %get-tuple-element.78.table_ref, bf16[128,512]{1,0:T(8,128)(2,1)S(1)} %copy-done.9, bf16[128,512]{1,0:T(8,128)(2,1)S(1)} %copy-done.4, bf16[128,512]{1,0:T(8,128)(2,1)S(1)} %copy-done.11, ...), custom_call_target="tpu_custom_call" | custom-call | flops 5637144576 | bytes 44040192 | tf_op jit(solution)/shard_map/cond/branch_2_fun/pallas_call | solution.py:571
  111.2 0.0 collective-permute-done.1
  111.2 0.0 copy-done.12
  111.2 0.1 add_convert_fusion
  111.3 0.7 slice_bitcast_fusion.2
Async XLA Ops:
  3.5 87.6 %copy-start.9 = (bf16[128,512]{1,0:T(8,128)(2,1)S(1)}, bf16[128,512]{1,0:T(8,128)(2,1)}, u32[]{:S(2)}) copy-start(bf16[128,512]{1,0:T(8,128)(2,1)} %get-tuple-element.71.refs_1_.refs_0_) | copy-start | bytes 393220 | tf_op jit(solution)/shard_map/cond
  3.5 87.6 %copy-start.11 = (bf16[128,512]{1,0:T(8,128)(2,1)S(1)}, bf16[128,512]{1,0:T(8,128)(2,1)}, u32[]{:S(2)}) copy-start(bf16[128,512]{1,0:T(8,128)(2,1)} %get-tuple-element.72.refs_2_) | copy-start | bytes 393220 | tf_op jit(solution)/shard_map/cond
  89.6 21.6 %collective-permute-start.1 = (bf16[2,128,512]{2,1,0:T(8,128)(2,1)}, bf16[2,128,512]{2,1,0:T(8,128)(2,1)S(1)}, u32[]{:S(2)}, u32[]{:S(2)}) collective-permute-start(bf16[2,128,512]{2,1,0:T(8,128)(2,1)} %get-tuple-element.77), channel_id=1, source_target_pairs={{0,1},{1,0},{2,3},{3,2},{4,5},{5,4},{6,7},{7,6},{8,9},{9,8},{10,11... | collective-permute-start | bytes 786440 | tf_op jit(solution)/shard_map/cond/branch_2_fun/ppermute | solution.py:1121
  91.2 2.6 %copy-start = (bf16[4,3,1792,128]{3,2,1,0:T(8,128)(2,1)S(1)}, bf16[4,3,1792,128]{3,2,1,0:T(8,128)(2,1)}, u32[]{:S(2)}) copy-start(bf16[4,3,1792,128]{3,2,1,0:T(8,128)(2,1)} %get-tuple-element.81.refs_4_) | copy-start | bytes 16515076 | tf_op jit(solution)/shard_map/cond
  93.7 0.9 copy-start.4
  94.6 0.9 copy-start.5
  95.5 15.7 %copy-start.12 = (f32[2,128,512]{2,1,0:T(8,128)S(1)}, f32[2,128,512]{2,1,0:T(8,128)}, u32[]{:S(2)}) copy-start(f32[2,128,512]{2,1,0:T(8,128)} %get-tuple-element.76) | copy-start | bytes 1572868 | tf_op jit(solution)/shard_map/cond
